TPU v7x, 256 devices: a whole 4x4x8 slice. The times are simulated.
256 devices in a mesh: section: 8 (over x, core), dp: 32 (over y, z).
Axes of the slice: x: 4, y: 4, z: 8, core: 2. Of those that a mesh axis runs over, the one named last changes fastest.
Arguments:
- inputs: bfloat16 [2, 32, 64, 1792], P(None, 'dp'), may hold values from -6 to 6
- cotangent: bfloat16 [2, 32, 64, 1792], P(None, 'dp'), may hold values from -180 to 180
- value_weight: bfloat16 [8, 1792, 1024], P('section', 'dp'), may hold values from -1 to 1
- output_weight: bfloat16 [8, 1024, 1792], P('section', 'dp'), may hold values from -1 to 1
- norm_gain: float32 [8, 1792], P('section'), may hold values from 0.5 to 2
- value_noise: float32 [8, 1792, 1024], P('section', 'dp'), may hold values from -6 to 6
- output_noise: float32 [8, 1024, 1792], P('section', 'dp'), may hold values from -6 to 6
Outputs:
- value_grad: float32 [8, 1792, 1024], P('section', 'dp')
- output_grad: float32 [8, 1024, 1792], P('section', 'dp')
All inputs are finite; a program needn't handle non-finite values.
Results may differ from a plain program's by a relative error of at most 0.018.
Values may be sent and summed in bfloat16 or wider, within the bound.
A program may use at most 64 MiB of HBM per device.

v0:
```python
import math
import jax
import jax.numpy as jnp
from jax import lax
from jax.sharding import Mesh, PartitionSpec as P


def from_behind(block, axis, distance):
    devices = range(lax.axis_size(axis))
    route = [(i - distance, i) for i in devices if i - distance in devices]
    return lax.ppermute(block, axis, route)


def norm_parts(current, gains):
    widened = current.astype(jnp.float32)
    inverse = lax.rsqrt(jnp.mean(widened * widened, axis=-1, keepdims=True) + 1e-06)
    normed = (widened * inverse * gains).astype(jnp.bfloat16)
    return (widened, inverse, normed)


def layer_forward(current, gains, value_matrix, output_matrix):
    widened, inverse, normed = norm_parts(current, gains)
    values = jnp.dot(normed, value_matrix, preferred_element_type=jnp.float32).astype(jnp.bfloat16)
    result = (widened + jnp.dot(values, output_matrix, preferred_element_type=jnp.float32)).astype(
        jnp.bfloat16
    )
    return (values, result)


def layer_backward(current, incoming, gains, value_matrix, output_matrix):
    widened, inverse, normed = norm_parts(current, gains)
    dvalues = jnp.dot(incoming, output_matrix.T, preferred_element_type=jnp.float32).astype(
        jnp.bfloat16
    )
    dnormed = jnp.dot(dvalues, value_matrix.T, preferred_element_type=jnp.float32) * gains
    centred = widened * inverse
    through = inverse * (dnormed - centred * jnp.mean(dnormed * centred, axis=-1, keepdims=True))
    before = (incoming.astype(jnp.float32) + through).astype(jnp.bfloat16)
    return (normed, dvalues, before)


def example_sums(left, right, seq_len):
    first = left.reshape(-1, seq_len, left.shape[-1])
    second = right.reshape(-1, seq_len, right.shape[-1])
    per_example = jnp.einsum("eth,etd->ehd", first, second, preferred_element_type=jnp.float32)
    return jnp.sum(per_example * per_example, axis=(1, 2))


def forward_chain(feed_rows, gains, value_matrix, output_matrix):
    section_count = lax.axis_size("section")
    section_place = lax.axis_index("section")
    micro_count, row_count, feature_width = feed_rows.shape
    head_width = value_matrix.shape[1]

    def forward_active_step(source):
        return layer_forward(source, gains, value_matrix, output_matrix)

    def forward_spare_step(source):
        return (
            jnp.zeros((row_count, head_width), jnp.bfloat16),
            jnp.zeros((row_count, feature_width), jnp.bfloat16),
        )

    def forward_time_step(counter, carried):
        incoming, kept_inputs, kept_values = carried
        which_micro = counter - section_place
        active = (which_micro >= 0) & (which_micro < micro_count)
        slot_index = jnp.clip(which_micro, 0, micro_count - 1)
        source = jnp.where(
            section_place == 0,
            lax.dynamic_index_in_dim(feed_rows, slot_index, 0, keepdims=False),
            incoming,
        )
        values, result = lax.cond(active, forward_active_step, forward_spare_step, source)
        old_inputs = lax.dynamic_index_in_dim(kept_inputs, slot_index, 0, keepdims=False)
        old_values = lax.dynamic_index_in_dim(kept_values, slot_index, 0, keepdims=False)
        kept_inputs = lax.dynamic_update_index_in_dim(
            kept_inputs, jnp.where(active, source, old_inputs), slot_index, 0
        )
        kept_values = lax.dynamic_update_index_in_dim(
            kept_values, jnp.where(active, values, old_values), slot_index, 0
        )
        incoming = from_behind(result, "section", 1)
        return (incoming, kept_inputs, kept_values)

    start_state = (
        jnp.zeros((row_count, feature_width), jnp.bfloat16),
        jnp.zeros((micro_count, row_count, feature_width), jnp.bfloat16),
        jnp.zeros((micro_count, row_count, head_width), jnp.bfloat16),
    )
    final_state = lax.fori_loop(0, section_count + micro_count - 1, forward_time_step, start_state)
    return (final_state[1], final_state[2])


def backward_chain(kept_inputs, kept_values, cot_rows, gains, value_matrix, output_matrix, seq_len):
    section_count = lax.axis_size("section")
    section_place = lax.axis_index("section")
    micro_count, row_count, feature_width = kept_inputs.shape
    head_width = kept_values.shape[-1]
    example_here = row_count // seq_len
    last_place = section_count - 1

    def backward_active_step(operands):
        inputs_here, values_here, grad_here = operands
        normed, dvalues, before = layer_backward(
            inputs_here, grad_here, gains, value_matrix, output_matrix
        )
        squares = example_sums(normed, dvalues, seq_len) + example_sums(
            values_here, grad_here, seq_len
        )
        return (before, dvalues, squares)

    def backward_spare_step(operands):
        return (
            jnp.zeros((row_count, feature_width), jnp.bfloat16),
            jnp.zeros((row_count, head_width), jnp.bfloat16),
            jnp.zeros((example_here,), jnp.float32),
        )

    def backward_time_step(counter, carried):
        incoming, kept_grads, kept_dvalues, squares_all = carried
        which_micro = counter - (last_place - section_place)
        active = (which_micro >= 0) & (which_micro < micro_count)
        slot_index = jnp.clip(which_micro, 0, micro_count - 1)
        grad_here = jnp.where(
            section_place == last_place,
            lax.dynamic_index_in_dim(cot_rows, slot_index, 0, keepdims=False),
            incoming,
        )
        inputs_here = lax.dynamic_index_in_dim(kept_inputs, slot_index, 0, keepdims=False)
        values_here = lax.dynamic_index_in_dim(kept_values, slot_index, 0, keepdims=False)
        before, dvalues, squares = lax.cond(
            active, backward_active_step, backward_spare_step, (inputs_here, values_here, grad_here)
        )
        old_grads = lax.dynamic_index_in_dim(kept_grads, slot_index, 0, keepdims=False)
        old_dvalues = lax.dynamic_index_in_dim(kept_dvalues, slot_index, 0, keepdims=False)
        old_squares = lax.dynamic_index_in_dim(squares_all, slot_index, 0, keepdims=False)
        kept_grads = lax.dynamic_update_index_in_dim(
            kept_grads, jnp.where(active, grad_here, old_grads), slot_index, 0
        )
        kept_dvalues = lax.dynamic_update_index_in_dim(
            kept_dvalues, jnp.where(active, dvalues, old_dvalues), slot_index, 0
        )
        squares_all = lax.dynamic_update_index_in_dim(
            squares_all, jnp.where(active, squares, old_squares), slot_index, 0
        )
        incoming = from_behind(before, "section", -1)
        return (incoming, kept_grads, kept_dvalues, squares_all)

    start_state = (
        jnp.zeros((row_count, feature_width), jnp.bfloat16),
        jnp.zeros((micro_count, row_count, feature_width), jnp.bfloat16),
        jnp.zeros((micro_count, row_count, head_width), jnp.bfloat16),
        jnp.zeros((micro_count, example_here), jnp.float32),
    )
    final_state = lax.fori_loop(0, section_count + micro_count - 1, backward_time_step, start_state)
    return (final_state[1], final_state[2], final_state[3])


DP = ("y", "z")


def gather_rows(shard):
    inner = lax.all_gather(shard, "z", axis=0, tiled=True)
    return lax.all_gather(inner, "y", axis=0, tiled=True)


def exchange_rows(shard):
    count = lax.axis_size(DP)
    copies = jnp.broadcast_to(shard[None], (count,) + shard.shape)
    parts = lax.all_to_all(copies, DP, 0, 0, tiled=False)
    return parts.reshape((-1,) + shard.shape[1:])


def scatter_in_stages(block):
    inner = lax.psum_scatter(block, "y", scatter_dimension=0, tiled=True)
    return lax.psum_scatter(inner, "z", scatter_dimension=0, tiled=True).astype(jnp.float32)


def scatter_by_exchange(block):
    count = lax.axis_size(DP)
    parts = block.reshape((count, block.shape[0] // count) + block.shape[1:])
    arrived = lax.all_to_all(parts, DP, 0, 0, tiled=False)
    return jnp.sum(arrived.astype(jnp.float32), axis=0)


def on_device(inputs, cotangent, value_weight, output_weight, norm_gain, value_noise, output_noise):
    micro_count, example_count, seq_len, feature_width = inputs.shape
    feed_rows = inputs.reshape(micro_count, example_count * seq_len, feature_width)
    cot_rows = cotangent.reshape(micro_count, example_count * seq_len, feature_width)
    value_matrix = gather_rows(value_weight[0])
    output_matrix = exchange_rows(output_weight[0])
    head_width = value_matrix.shape[1]
    gains = norm_gain[0]
    kept_inputs, kept_values = forward_chain(feed_rows, gains, value_matrix, output_matrix)
    kept_grads, kept_dvalues, partial_squares = backward_chain(
        kept_inputs, kept_values, cot_rows, gains, value_matrix, output_matrix, seq_len
    )
    total_squares = lax.psum(partial_squares, "section")
    clip_weight = 1.0 / (jnp.sqrt(total_squares) + 0.01)
    token_weight = jnp.repeat(clip_weight, seq_len, axis=1)[:, :, None]
    scaled_dvalues = (
        (kept_dvalues.astype(jnp.float32) * token_weight)
        .astype(jnp.bfloat16)
        .reshape(-1, head_width)
    )
    scaled_grads = (
        (kept_grads.astype(jnp.float32) * token_weight)
        .astype(jnp.bfloat16)
        .reshape(-1, feature_width)
    )
    unused_wide, unused_inverse, normed_rows = norm_parts(
        kept_inputs.reshape(-1, feature_width), gains
    )
    value_rows = kept_values.reshape(-1, head_width)
    columns = normed_rows
    value_part = scatter_in_stages(
        lax.dot_general(
            columns, scaled_dvalues, (((0,), (0,)), ((), ())), preferred_element_type=jnp.float32
        ).astype(jnp.bfloat16)
    )
    columns = value_rows
    output_part = scatter_by_exchange(
        lax.dot_general(
            columns, scaled_grads, (((0,), (0,)), ((), ())), preferred_element_type=jnp.float32
        ).astype(jnp.bfloat16)
    )
    grad_scale = math.sqrt(feature_width * head_width)
    value_grad = (value_part * grad_scale + value_noise[0])[None]
    output_grad = (output_part * grad_scale + output_noise[0])[None]
    return (value_grad, output_grad)


def split_dp(mesh):
    devices = mesh.devices
    sections, count = devices.shape
    try:
        across = len({d.coords[1] for d in devices[0]})
    except (AttributeError, IndexError, TypeError):
        across = 1
    if across < 1 or count % across:
        across = 1
    return Mesh(devices.reshape(sections, across, count // across), ("section",) + DP)


def solution(mesh):
    grid = split_dp(mesh)
    return jax.shard_map(
        on_device,
        mesh=grid,
        in_specs=(
            P(None, DP, None, None),
            P(None, DP, None, None),
            P("section", DP, None),
            P("section", DP, None),
            P("section", None),
            P("section", DP, None),
            P("section", DP, None),
        ),
        out_specs=(P("section", DP, None), P("section", DP, None)),
        check_vma=False,
    )
```

profile of v0, /device:TPU:2, one launch (start us, length us, event | category | flops | bytes accessed | tf_op | source)
XLA Modules:
  0.0 588.7 jit_solution(12497531110454642045)
XLA Ops:
  7.2 3.2 broadcast_in_dim.63
  10.4 11.7 %all-to-all-start = ((bf16[32,32,1792]{2,1,0:T(8,128)(2,1)}), bf16[32,32,1792]{2,1,0:T(8,128)(2,1)}, u32[]{:S(2)}, u32[]{:S(2)}) async-start(bf16[32,32,1792]{2,1,0:T(8,128)(2,1)} %broadcast_in_dim.63), calls=%async_computation | async-start | bytes 7340032 | tf_op jit(solution)/shard_map/all_to_all | solution.py:171
  22.2 105.7 %all-gather = bf16[1,448,1024]{2,1,0:T(8,128)(2,1)} all-gather(bf16[1,56,1024]{2,1,0:T(8,128)(2,1)S(1)} %copy-done.7), channel_id=2, replica_groups=mesh['section'=8,'y'=4,'z'=8] {'z'}, dimensions={1}, use_global_device_ids=true | all-gather | bytes 1032192 | tf_op jit(solution)/shard_map/all_gather | solution.py:164
  128.0 45.0 %all-gather.4.cloned.1.call-done = bf16[1,1792,1024]{2,1,0:T(8,128)(2,1)} async-done(((bf16[1,448,1024]{2,1,0:T(8,128)(2,1)}), bf16[1,1792,1024]{2,1,0:T(8,128)(2,1)}) %all-gather.4.cloned.1.call-update) | async-done | bytes 3670032 | tf_op jit(solution)/shard_map/all_gather | solution.py:165
  173.1 91.9 %while.39 = (s32[]{:T(128)}, bf16[64,1792]{1,0:T(8,128)(2,1)S(1)}, bf16[2,64,1792]{2,1,0:T(8,128)(2,1)S(1)}, bf16[2,64,1024]{2,1,0:T(8,128)(2,1)S(1)}, s32[]{:T(...) while((s32[]{:T(128)}, bf16[64,1792]{1,0:T(8,128)(2,1)S(1)}, ...), condition=%wide.region_4.5_spmd, body=%wide.region_0.4_spmd.sunk | while | flops 471269440 | bytes 11721002 | solution.py:91
  173.9 1.9 collective-permute-start
  175.9 5.3 collective-permute-done
  182.1 1.9 collective-permute-start
  184.1 11.0 %collective-permute-done = bf16[64,1792]{1,0:T(8,128)(2,1)S(1)} collective-permute-done((bf16[64,1792]{1,0:T(8,128)(2,1)S(1)}, bf16[64,1792]{1,0:T(8,128)(2,1)S(1)}, u32[]{:S(2)}, u32[]{:S(2)}) %collective-permute-start) | collective-permute-done | bytes 229408 | tf_op jit(solution)/shard_map/while/body/eval_jaxpr/ppermute | solution.py:11
  195.2 6.6 %conditional.4 = (bf16[64,1024]{1,0:T(8,128)(2,1)}, bf16[64,1792]{1,0:T(8,128)(2,1)S(1)}) conditional(s32[]{:T(128)} %convert_element_type.145, () %tuple.96, (bf16[64,1792]{1,0:T(8,128)(2,1)S(1)}, f32[1,1792]{1,0:T(1,128)S(1)}, bf16[1792,1024]{1,0:T(8,128)(2,1)}, bf16[1024,1792]{1,0:T(8,128)(2,1)}) %tuple.97), branch_computations={%region_1.1_spmd, %region_2.3_spmd} | conditional | flops 470974528 | bytes 8542228 | solution.py:74
  195.4 3.5 convolution_convert_fusion
  198.9 2.9 fusion
  201.8 1.9 collective-permute-start
  204.7 4.4 collective-permute-done
  209.2 6.6 %conditional.4 = (bf16[64,1024]{1,0:T(8,128)(2,1)}, bf16[64,1792]{1,0:T(8,128)(2,1)S(1)}) conditional(s32[]{:T(128)} %convert_element_type.145, () %tuple.96, (bf16[64,1792]{1,0:T(8,128)(2,1)S(1)}, f32[1,1792]{1,0:T(1,128)S(1)}, bf16[1792,1024]{1,0:T(8,128)(2,1)}, bf16[1024,1792]{1,0:T(8,128)(2,1)}) %tuple.97), branch_computations={%region_1.1_spmd, %region_2.3_spmd} | conditional | flops 470974528 | bytes 8542228 | solution.py:74
  209.4 3.5 convolution_convert_fusion
  212.9 2.9 fusion
  215.8 1.9 collective-permute-start
  218.7 4.4 collective-permute-done
  224.0 3.8 collective-permute-start
  227.9 3.4 collective-permute-done
  232.1 1.9 collective-permute-start
  234.1 5.3 collective-permute-done
  240.3 7.3 %collective-permute-start = (bf16[64,1792]{1,0:T(8,128)(2,1)S(1)}, bf16[64,1792]{1,0:T(8,128)(2,1)S(1)}, u32[]{:S(2)}, u32[]{:S(2)}) collective-permute-start(bf16[64,1792]{1,0:T(8,128)(2,1)S(1)} %get-tuple-element.751), channel_id=1, source_target_pairs={{0,32},{32,64},{64,96},{96,128},{128,160},{160,192},{192,224},{1,3... | collective-permute-start | bytes 688136 | tf_op jit(solution)/shard_map/while/body/eval_jaxpr/ppermute | solution.py:11
  249.5 6.2 %collective-permute-start = (bf16[64,1792]{1,0:T(8,128)(2,1)S(1)}, bf16[64,1792]{1,0:T(8,128)(2,1)S(1)}, u32[]{:S(2)}, u32[]{:S(2)}) collective-permute-start(bf16[64,1792]{1,0:T(8,128)(2,1)S(1)} %get-tuple-element.751), channel_id=1, source_target_pairs={{0,32},{32,64},{64,96},{96,128},{128,160},{160,192},{192,224},{1,3... | collective-permute-start | bytes 688136 | tf_op jit(solution)/shard_map/while/body/eval_jaxpr/ppermute | solution.py:11
  257.6 6.2 %collective-permute-start = (bf16[64,1792]{1,0:T(8,128)(2,1)S(1)}, bf16[64,1792]{1,0:T(8,128)(2,1)S(1)}, u32[]{:S(2)}, u32[]{:S(2)}) collective-permute-start(bf16[64,1792]{1,0:T(8,128)(2,1)S(1)} %get-tuple-element.751), channel_id=1, source_target_pairs={{0,32},{32,64},{64,96},{96,128},{128,160},{160,192},{192,224},{1,3... | collective-permute-start | bytes 688136 | tf_op jit(solution)/shard_map/while/body/eval_jaxpr/ppermute | solution.py:11
  265.3 172.9 %while.40 = (s32[]{:T(128)}, bf16[64,1792]{1,0:T(8,128)(2,1)S(1)}, bf16[2,64,1792]{2,1,0:T(8,128)(2,1)S(1)}, bf16[2,64,1024]{2,1,0:T(8,128)(2,1)S(1)}, f32[2,1]{...) while((s32[]{:T(128)}, bf16[64,1792]{1,0:T(8,128)(2,1)S(1)}, ...), condition=%wide.region_13.14_spmd, body=%wide.region_6.0_spmd.sunk | while | flops 949518400 | bytes 14876903 | solution.py:156
  265.5 1.9 collective-permute-start.1
  268.8 3.9 collective-permute-done.1
  272.9 2.0 collective-permute-start.1
  276.3 5.7 collective-permute-done.1
  282.2 1.9 collective-permute-start.1
  285.5 4.1 collective-permute-done.1
  289.8 1.9 collective-permute-start.1
  293.1 4.7 collective-permute-done.1
  297.9 1.9 collective-permute-start.1
  301.2 66.8 %collective-permute-done.1 = bf16[64,1792]{1,0:T(8,128)(2,1)S(1)} collective-permute-done((bf16[64,1792]{1,0:T(8,128)(2,1)S(1)}, bf16[64,1792]{1,0:T(8,128)(2,1)S(1)}, u32[]{:S(2)}, u32[]{:S(2)}) %collective-permute-start.1) | collective-permute-done | bytes 229408 | tf_op jit(solution)/shard_map/while/body/eval_jaxpr/ppermute | solution.py:11
  368.1 14.0 %conditional.5 = (bf16[64,1792]{1,0:T(8,128)(2,1)S(1)}, bf16[64,1024]{1,0:T(8,128)(2,1)S(1)}, f32[1]{0:T(128)}) conditional(s32[]{:T(128)} %convert_element_type.146, () %tuple.100, (bf16[64,1792]{1,0:T(8,128)(2,1)S(1)}, bf16[2,64,1792]{2,1,0:T(8,128)(2,1)S(1)}, s32[]{:T(128)}, bf16[1024,1792]{1,0:T(8,128)(2,1)}, bf16[1792,1024]{1,0:T(8,128)(2,1)}, ...), branch_computations={%region_7.7_spmd, %region_8.12_spmd} | conditional | flops 949223488 | bytes 11698044 | solution.py:132
  368.3 3.3 convolution_convert_fusion.1
  371.6 3.4 fusion.10
  375.3 2.8 multiply_reduce_fusion.1
  378.1 2.8 multiply_reduce_fusion
  382.2 1.9 collective-permute-start.1
  385.5 4.1 collective-permute-done.1
  389.6 14.0 %conditional.5 = (bf16[64,1792]{1,0:T(8,128)(2,1)S(1)}, bf16[64,1024]{1,0:T(8,128)(2,1)S(1)}, f32[1]{0:T(128)}) conditional(s32[]{:T(128)} %convert_element_type.146, () %tuple.100, (bf16[64,1792]{1,0:T(8,128)(2,1)S(1)}, bf16[2,64,1792]{2,1,0:T(8,128)(2,1)S(1)}, s32[]{:T(128)}, bf16[1024,1792]{1,0:T(8,128)(2,1)}, bf16[1792,1024]{1,0:T(8,128)(2,1)}, ...), branch_computations={%region_7.7_spmd, %region_8.12_spmd} | conditional | flops 949223488 | bytes 11698044 | solution.py:132
  389.8 3.3 convolution_convert_fusion.1
  393.1 3.4 fusion.10
  396.8 2.8 multiply_reduce_fusion.1
  399.6 2.8 multiply_reduce_fusion
  403.7 1.9 collective-permute-start.1
  407.0 2.1 collective-permute-done.1
  409.3 17.8 %collective-permute-start.1 = (bf16[64,1792]{1,0:T(8,128)(2,1)S(1)}, bf16[64,1792]{1,0:T(8,128)(2,1)S(1)}, u32[]{:S(2)}, u32[]{:S(2)}) collective-permute-start(bf16[64,1792]{1,0:T(8,128)(2,1)S(1)} %get-tuple-element.768), channel_id=1, source_target_pairs={{32,0},{64,32},{96,64},{128,96},{160,128},{192,160},{224,192},{33,... | collective-permute-start | bytes 688136 | tf_op jit(solution)/shard_map/while/body/eval_jaxpr/ppermute | solution.py:11
  428.5 2.1 collective-permute-done.1
  430.8 3.8 collective-permute-start.1
  436.1 2.1 collective-permute-done.1
  438.2 18.2 %psum.7 = f32[2,1]{0,1:T(1,128)S(1)} all-reduce(f32[2,1]{0,1:T(1,128)S(1)} %get-tuple-element.560), channel_id=1, replica_groups=mesh['section'=8,'y'=4,'z'=8] {'section'}, use_global_device_ids=true, to_apply=%region_14.15 | all-reduce | flops 2 | bytes 16 | tf_op jit(solution)/shard_map/psum | solution.py:199
  456.4 3.1 bitcast_convert_fusion.1
  459.5 3.1 bitcast_convert_fusion
  462.6 8.9 %all-to-all-start.1 = ((bf16[32,32,1792]{2,1,0:T(8,128)(2,1)}), bf16[32,32,1792]{2,1,0:T(8,128)(2,1)}, u32[]{:S(2)}, u32[]{:S(2)}) async-start(bf16[32,32,1792]{2,1,0:T(8,128)(2,1)} %bitcast.99), calls=%async_computation.3 | async-start | bytes 7340032 | tf_op jit(solution)/shard_map/all_to_all | solution.py:183
  471.6 62.9 %reduce-scatter.3.cloned.1.call-done = bf16[448,1024]{1,0:T(8,128)(2,1)} async-done(((bf16[1792,1024]{1,0:T(8,128)(2,1)}), bf16[448,1024]{1,0:T(8,128)(2,1)}) %reduce-scatter.3.cloned.1.call-update) | async-done | bytes 917520 | tf_op jit(solution)/shard_map/reduce_scatter | solution.py:176
  534.6 21.4 %all-to-all-done.1 = bf16[32,32,1792]{2,1,0:T(8,128)(2,1)} async-done(((bf16[32,32,1792]{2,1,0:T(8,128)(2,1)}), bf16[32,32,1792]{2,1,0:T(8,128)(2,1)}, u32[]{:S(2)}, u32[]{:S(2)}) %all-to-all-start.1) | async-done | bytes 3670048 | tf_op jit(solution)/shard_map/all_to_all | solution.py:183
  556.0 2.6 convert_reduce_fusion
  559.3 21.3 %reduce-scatter.5.cloned.1.call-done = bf16[56,1024]{1,0:T(8,128)(2,1)} async-done(((bf16[448,1024]{1,0:T(8,128)(2,1)}), bf16[56,1024]{1,0:T(8,128)(2,1)}) %reduce-scatter.5.cloned.1.call-update) | async-done | bytes 114704 | tf_op jit(solution)/shard_map/reduce_scatter | solution.py:177
  580.6 1.6 fusion.34
  (190 shorter events, 26.8 us)
Async XLA Ops:
  10.4 11.8 %copy-start.7 = (bf16[1,56,1024]{2,1,0:T(8,128)(2,1)S(1)}, bf16[1,56,1024]{2,1,0:T(8,128)(2,1)}, u32[]{:S(2)}) copy-start(bf16[1,56,1024]{2,1,0:T(8,128)(2,1)} %param.17) | copy-start | bytes 344068
  10.4 117.5 %copy-start.4 = (f32[1,1792]{1,0:T(1,128)S(1)}, f32[1,1792]{1,0:T(1,128)}, u32[]{:S(2)}) copy-start(f32[1,1792]{1,0:T(1,128)} %param.19) | copy-start | bytes 21508
  10.4 162.6 %copy-start.2 = (bf16[2,1,64,1792]{3,2,1,0:T(8,128)(2,1)S(1)}, bf16[2,1,64,1792]{3,2,1,0:T(8,128)(2,1)}, u32[]{:S(2)}) copy-start(bf16[2,1,64,1792]{3,2,1,0:T(8,128)(2,1)} %param.15) | copy-start | bytes 1376260
  10.4 162.5 %all-to-all-start = ((bf16[32,32,1792]{2,1,0:T(8,128)(2,1)}), bf16[32,32,1792]{2,1,0:T(8,128)(2,1)}, u32[]{:S(2)}, u32[]{:S(2)}) async-start(bf16[32,32,1792]{2,1,0:T(8,128)(2,1)} %broadcast_in_dim.63), calls=%async_computation | async-start | bytes 7340032 | tf_op jit(solution)/shard_map/all_to_all | solution.py:171
  22.1 150.8 %all-gather.4.cloned.1.call-start = ((), (), s32[]{:S(2)}) async-start(), calls=%async_computation.6 | async-start | bytes 4587520 | tf_op jit(solution)/shard_map/all_gather | solution.py:165
  127.9 406.7 %reduce-scatter.3.cloned.1.call-start = ((), (), s32[]{:S(2)}) async-start(), calls=%async_computation.4 | async-start | bytes 4587520 | tf_op jit(solution)/shard_map/reduce_scatter | solution.py:176
  173.0 92.2 %copy-start.3 = (bf16[2,1,64,1792]{3,2,1,0:T(8,128)(2,1)S(1)}, bf16[2,1,64,1792]{3,2,1,0:T(8,128)(2,1)}, u32[]{:S(2)}) copy-start(bf16[2,1,64,1792]{3,2,1,0:T(8,128)(2,1)} %param.16) | copy-start | bytes 1376260
  173.9 7.3 %collective-permute-start = (bf16[64,1792]{1,0:T(8,128)(2,1)S(1)}, bf16[64,1792]{1,0:T(8,128)(2,1)S(1)}, u32[]{:S(2)}, u32[]{:S(2)}) collective-permute-start(bf16[64,1792]{1,0:T(8,128)(2,1)S(1)} %get-tuple-element.751), channel_id=1, source_target_pairs={{0,32},{32,64},{64,96},{96,128},{128,160},{160,192},{192,224},{1,3... | collective-permute-start | bytes 688136 | tf_op jit(solution)/shard_map/while/body/eval_jaxpr/ppermute | solution.py:11
  182.1 13.0 %collective-permute-start = (bf16[64,1792]{1,0:T(8,128)(2,1)S(1)}, bf16[64,1792]{1,0:T(8,128)(2,1)S(1)}, u32[]{:S(2)}, u32[]{:S(2)}) collective-permute-start(bf16[64,1792]{1,0:T(8,128)(2,1)S(1)} %get-tuple-element.751), channel_id=1, source_target_pairs={{0,32},{32,64},{64,96},{96,128},{128,160},{160,192},{192,224},{1,3... | collective-permute-start | bytes 688136 | tf_op jit(solution)/shard_map/while/body/eval_jaxpr/ppermute | solution.py:11
  201.8 7.3 %collective-permute-start = (bf16[64,1792]{1,0:T(8,128)(2,1)S(1)}, bf16[64,1792]{1,0:T(8,128)(2,1)S(1)}, u32[]{:S(2)}, u32[]{:S(2)}) collective-permute-start(bf16[64,1792]{1,0:T(8,128)(2,1)S(1)} %get-tuple-element.751), channel_id=1, source_target_pairs={{0,32},{32,64},{64,96},{96,128},{128,160},{160,192},{192,224},{1,3... | collective-permute-start | bytes 688136 | tf_op jit(solution)/shard_map/while/body/eval_jaxpr/ppermute | solution.py:11
  215.8 7.3 %collective-permute-start = (bf16[64,1792]{1,0:T(8,128)(2,1)S(1)}, bf16[64,1792]{1,0:T(8,128)(2,1)S(1)}, u32[]{:S(2)}, u32[]{:S(2)}) collective-permute-start(bf16[64,1792]{1,0:T(8,128)(2,1)S(1)} %get-tuple-element.751), channel_id=1, source_target_pairs={{0,32},{32,64},{64,96},{96,128},{128,160},{160,192},{192,224},{1,3... | collective-permute-start | bytes 688136 | tf_op jit(solution)/shard_map/while/body/eval_jaxpr/ppermute | solution.py:11
  224.0 7.3 %collective-permute-start = (bf16[64,1792]{1,0:T(8,128)(2,1)S(1)}, bf16[64,1792]{1,0:T(8,128)(2,1)S(1)}, u32[]{:S(2)}, u32[]{:S(2)}) collective-permute-start(bf16[64,1792]{1,0:T(8,128)(2,1)S(1)} %get-tuple-element.751), channel_id=1, source_target_pairs={{0,32},{32,64},{64,96},{96,128},{128,160},{160,192},{192,224},{1,3... | collective-permute-start | bytes 688136 | tf_op jit(solution)/shard_map/while/body/eval_jaxpr/ppermute | solution.py:11
  232.1 7.3 %collective-permute-start = (bf16[64,1792]{1,0:T(8,128)(2,1)S(1)}, bf16[64,1792]{1,0:T(8,128)(2,1)S(1)}, u32[]{:S(2)}, u32[]{:S(2)}) collective-permute-start(bf16[64,1792]{1,0:T(8,128)(2,1)S(1)} %get-tuple-element.751), channel_id=1, source_target_pairs={{0,32},{32,64},{64,96},{96,128},{128,160},{160,192},{192,224},{1,3... | collective-permute-start | bytes 688136 | tf_op jit(solution)/shard_map/while/body/eval_jaxpr/ppermute | solution.py:11
  240.3 8.4 %collective-permute-start = (bf16[64,1792]{1,0:T(8,128)(2,1)S(1)}, bf16[64,1792]{1,0:T(8,128)(2,1)S(1)}, u32[]{:S(2)}, u32[]{:S(2)}) collective-permute-start(bf16[64,1792]{1,0:T(8,128)(2,1)S(1)} %get-tuple-element.751), channel_id=1, source_target_pairs={{0,32},{32,64},{64,96},{96,128},{128,160},{160,192},{192,224},{1,3... | collective-permute-start | bytes 688136 | tf_op jit(solution)/shard_map/while/body/eval_jaxpr/ppermute | solution.py:11
  249.5 7.3 %collective-permute-start = (bf16[64,1792]{1,0:T(8,128)(2,1)S(1)}, bf16[64,1792]{1,0:T(8,128)(2,1)S(1)}, u32[]{:S(2)}, u32[]{:S(2)}) collective-permute-start(bf16[64,1792]{1,0:T(8,128)(2,1)S(1)} %get-tuple-element.751), channel_id=1, source_target_pairs={{0,32},{32,64},{64,96},{96,128},{128,160},{160,192},{192,224},{1,3... | collective-permute-start | bytes 688136 | tf_op jit(solution)/shard_map/while/body/eval_jaxpr/ppermute | solution.py:11
  257.6 7.3 %collective-permute-start = (bf16[64,1792]{1,0:T(8,128)(2,1)S(1)}, bf16[64,1792]{1,0:T(8,128)(2,1)S(1)}, u32[]{:S(2)}, u32[]{:S(2)}) collective-permute-start(bf16[64,1792]{1,0:T(8,128)(2,1)S(1)} %get-tuple-element.751), channel_id=1, source_target_pairs={{0,32},{32,64},{64,96},{96,128},{128,160},{160,192},{192,224},{1,3... | collective-permute-start | bytes 688136 | tf_op jit(solution)/shard_map/while/body/eval_jaxpr/ppermute | solution.py:11
  265.5 7.2 %collective-permute-start.1 = (bf16[64,1792]{1,0:T(8,128)(2,1)S(1)}, bf16[64,1792]{1,0:T(8,128)(2,1)S(1)}, u32[]{:S(2)}, u32[]{:S(2)}) collective-permute-start(bf16[64,1792]{1,0:T(8,128)(2,1)S(1)} %get-tuple-element.768), channel_id=1, source_target_pairs={{32,0},{64,32},{96,64},{128,96},{160,128},{192,160},{224,192},{33,... | collective-permute-start | bytes 688136 | tf_op jit(solution)/shard_map/while/body/eval_jaxpr/ppermute | solution.py:11
  272.9 9.1 %collective-permute-start.1 = (bf16[64,1792]{1,0:T(8,128)(2,1)S(1)}, bf16[64,1792]{1,0:T(8,128)(2,1)S(1)}, u32[]{:S(2)}, u32[]{:S(2)}) collective-permute-start(bf16[64,1792]{1,0:T(8,128)(2,1)S(1)} %get-tuple-element.768), channel_id=1, source_target_pairs={{32,0},{64,32},{96,64},{128,96},{160,128},{192,160},{224,192},{33,... | collective-permute-start | bytes 688136 | tf_op jit(solution)/shard_map/while/body/eval_jaxpr/ppermute | solution.py:11
  282.2 7.3 %collective-permute-start.1 = (bf16[64,1792]{1,0:T(8,128)(2,1)S(1)}, bf16[64,1792]{1,0:T(8,128)(2,1)S(1)}, u32[]{:S(2)}, u32[]{:S(2)}) collective-permute-start(bf16[64,1792]{1,0:T(8,128)(2,1)S(1)} %get-tuple-element.768), channel_id=1, source_target_pairs={{32,0},{64,32},{96,64},{128,96},{160,128},{192,160},{224,192},{33,... | collective-permute-start | bytes 688136 | tf_op jit(solution)/shard_map/while/body/eval_jaxpr/ppermute | solution.py:11
  289.8 8.0 %collective-permute-start.1 = (bf16[64,1792]{1,0:T(8,128)(2,1)S(1)}, bf16[64,1792]{1,0:T(8,128)(2,1)S(1)}, u32[]{:S(2)}, u32[]{:S(2)}) collective-permute-start(bf16[64,1792]{1,0:T(8,128)(2,1)S(1)} %get-tuple-element.768), channel_id=1, source_target_pairs={{32,0},{64,32},{96,64},{128,96},{160,128},{192,160},{224,192},{33,... | collective-permute-start | bytes 688136 | tf_op jit(solution)/shard_map/while/body/eval_jaxpr/ppermute | solution.py:11
  297.9 70.1 %collective-permute-start.1 = (bf16[64,1792]{1,0:T(8,128)(2,1)S(1)}, bf16[64,1792]{1,0:T(8,128)(2,1)S(1)}, u32[]{:S(2)}, u32[]{:S(2)}) collective-permute-start(bf16[64,1792]{1,0:T(8,128)(2,1)S(1)} %get-tuple-element.768), channel_id=1, source_target_pairs={{32,0},{64,32},{96,64},{128,96},{160,128},{192,160},{224,192},{33,... | collective-permute-start | bytes 688136 | tf_op jit(solution)/shard_map/while/body/eval_jaxpr/ppermute | solution.py:11
  371.6 6.5 %copy-start = (bf16[64,1024]{1,0:T(8,128)(2,1)}, bf16[64,1024]{1,0:T(8,128)(2,1)S(1)}, u32[]{:S(2)}) copy-start(bf16[64,1024]{1,0:T(8,128)(2,1)S(1)} %convolution_convert_fusion.1) | copy-start | bytes 393220 | tf_op jit(solution)/shard_map/while/body/eval_jaxpr/cond
  378.1 4.1 copy-start.1
  382.2 7.3 %collective-permute-start.1 = (bf16[64,1792]{1,0:T(8,128)(2,1)S(1)}, bf16[64,1792]{1,0:T(8,128)(2,1)S(1)}, u32[]{:S(2)}, u32[]{:S(2)}) collective-permute-start(bf16[64,1792]{1,0:T(8,128)(2,1)S(1)} %get-tuple-element.768), channel_id=1, source_target_pairs={{32,0},{64,32},{96,64},{128,96},{160,128},{192,160},{224,192},{33,... | collective-permute-start | bytes 688136 | tf_op jit(solution)/shard_map/while/body/eval_jaxpr/ppermute | solution.py:11
  393.1 6.5 %copy-start = (bf16[64,1024]{1,0:T(8,128)(2,1)}, bf16[64,1024]{1,0:T(8,128)(2,1)S(1)}, u32[]{:S(2)}) copy-start(bf16[64,1024]{1,0:T(8,128)(2,1)S(1)} %convolution_convert_fusion.1) | copy-start | bytes 393220 | tf_op jit(solution)/shard_map/while/body/eval_jaxpr/cond
  399.6 4.1 copy-start.1
  403.7 5.4 collective-permute-start.1
  409.3 21.3 %collective-permute-start.1 = (bf16[64,1792]{1,0:T(8,128)(2,1)S(1)}, bf16[64,1792]{1,0:T(8,128)(2,1)S(1)}, u32[]{:S(2)}, u32[]{:S(2)}) collective-permute-start(bf16[64,1792]{1,0:T(8,128)(2,1)S(1)} %get-tuple-element.768), channel_id=1, source_target_pairs={{32,0},{64,32},{96,64},{128,96},{160,128},{192,160},{224,192},{33,... | collective-permute-start | bytes 688136 | tf_op jit(solution)/shard_map/while/body/eval_jaxpr/ppermute | solution.py:11
  430.8 7.3 %collective-permute-start.1 = (bf16[64,1792]{1,0:T(8,128)(2,1)S(1)}, bf16[64,1792]{1,0:T(8,128)(2,1)S(1)}, u32[]{:S(2)}, u32[]{:S(2)}) collective-permute-start(bf16[64,1792]{1,0:T(8,128)(2,1)S(1)} %get-tuple-element.768), channel_id=1, source_target_pairs={{32,0},{64,32},{96,64},{128,96},{160,128},{192,160},{224,192},{33,... | collective-permute-start | bytes 688136 | tf_op jit(solution)/shard_map/while/body/eval_jaxpr/ppermute | solution.py:11
  462.6 93.4 %all-to-all-start.1 = ((bf16[32,32,1792]{2,1,0:T(8,128)(2,1)}), bf16[32,32,1792]{2,1,0:T(8,128)(2,1)}, u32[]{:S(2)}, u32[]{:S(2)}) async-start(bf16[32,32,1792]{2,1,0:T(8,128)(2,1)} %bitcast.99), calls=%async_computation.3 | async-start | bytes 7340032 | tf_op jit(solution)/shard_map/all_to_all | solution.py:183
  471.6 87.0 %copy-start.6 = (f32[1,32,1792]{2,1,0:T(8,128)S(1)}, f32[1,32,1792]{2,1,0:T(8,128)}, u32[]{:S(2)}) copy-start(f32[1,32,1792]{2,1,0:T(8,128)} %param.21) | copy-start | bytes 688132
  471.6 109.0 %copy-start.5 = (f32[1,56,1024]{2,1,0:T(8,128)S(1)}, f32[1,56,1024]{2,1,0:T(8,128)}, u32[]{:S(2)}) copy-start(f32[1,56,1024]{2,1,0:T(8,128)} %param.20) | copy-start | bytes 688132
  471.6 109.0 %reduce-scatter.5.cloned.1.call-start = ((), (), s32[]{:S(2)}) async-start(), calls=%async_computation.5 | async-start | bytes 1032192 | tf_op jit(solution)/shard_map/reduce_scatter | solution.py:177
Sparse Core Ops, SparseCore 0:
  128.0 44.8 all-gather.3
  459.7 74.8 reduce-scatter.2
  537.1 43.4 reduce-scatter.4
where the time goes:
time: 590 us; the launch traced here: 589 us
  waiting for transfers between devices  283 us (48%)
  blocking collectives  124 us (21%)
  starting transfers between devices  89.1 us (15%)
  matrix products  43.4 us (7%)
  local copies, waits for them, and re-layouts  15 us (3%)
  between operations  13.9 us (2%)
  other arithmetic  10.6 us (2%)
  loops' own time  9.87 us (2%)
    ppermute x18, waiting for transfers between devices, from_behind(): return lax.ppermute(block, axis, route)  132 us
    all_gather x1, blocking collectives, gather_rows(): inner = lax.all_gather(shard, 'z', axis=0, tiled=True)  106 us
    ppermute x18, starting transfers between devices, from_behind(): return lax.ppermute(block, axis, route)  68.3 us
    reduce_scatter x1, waiting for transfers between devices, scatter_in_stages(): inner = lax.psum_scatter(block, 'y', scatter_dimension=0, tiled=True)  62.9 us
    all_gather x1, waiting for transfers between devices, gather_rows(): return lax.all_gather(inner, 'y', axis=0, tiled=True)  45 us
    all_to_all x1, waiting for transfers between devices, scatter_by_exchange(): arrived = lax.all_to_all(parts, DP, 0, 0, tiled=False)  21.4 us
    reduce_scatter x1, waiting for transfers between devices, scatter_in_stages(): lax.psum_scatter(inner, 'z', scatter_dimension=0, tiled=True)  21.3 us
    psum x1, blocking collectives, on_device(): total_squares = lax.psum(partial_squares, 'section')  18.2 us
  transfers between devices with their start and end apart: 23, of which 22 were waited for; matrix products, arithmetic and copies ran while one was open for 3% of the time, Pallas kernels for 0%

commit v1 on v0

--- a/solution.py
+++ b/solution.py
@@ -161,7 +161,19 @@
 
 
 def gather_rows(shard):
-    inner = lax.all_gather(shard, "z", axis=0, tiled=True)
+
+    def supply_block_in(w_in, dim_at):
+        return jnp.concatenate(
+            jax.lax.all_to_all(
+                jnp.stack([w_in] * jax.lax.axis_size("z")),
+                axis_name="z",
+                split_axis=0,
+                concat_axis=0,
+            ),
+            axis=dim_at,
+        )
+
+    inner = supply_block_in(shard, dim_at=0)
     return lax.all_gather(inner, "y", axis=0, tiled=True)
 
 

time: 590 us -> 550 us (0.932)
  blocking collectives: 124 us -> 52.5 us
  waiting for transfers between devices: 283 us -> 323 us
  starting transfers between devices: 89.1 us -> 79.2 us
    all_gather x1 -> x0, blocking collectives: 106 us -> none  [gather_rows(): inner = lax.all_gather(shard, 'z', axis=0, tiled=True)]
    all_to_all x1, waiting for transfers between devices: 0.01 us -> 84.7 us  [exchange_rows(): parts = lax.all_to_all(copies, DP, 0, 0, tiled=False)]
    all_gather x1, waiting for transfers between devices: 45 us -> 0.01 us  [gather_rows(): return lax.all_gather(inner, 'y', axis=0, tiled=True)]
    all_to_all x0 -> x1, blocking collectives: none -> 34.3 us  [supply_block_in(): jax.lax.all_to_all(jnp.stack([w_in] * jax.lax.axis_size('z')), axis_name=...]
    all_to_all x1, starting transfers between devices: 11.7 us -> 5.1 us  [exchange_rows(): parts = lax.all_to_all(copies, DP, 0, 0, tiled=False)]
where the time goes in v1:
time: 550 us; the launch traced here: 549 us
  waiting for transfers between devices  323 us (59%)
  starting transfers between devices  79.2 us (14%)
  blocking collectives  52.5 us (10%)
  matrix products  43.4 us (8%)
  local copies, waits for them, and re-layouts  16 us (3%)
  between operations  13.9 us (3%)
  other arithmetic  10.6 us (2%)
  loops' own time  9.87 us (2%)
    ppermute x18, waiting for transfers between devices, from_behind(): return lax.ppermute(block, axis, route)  132 us
    all_to_all x1, waiting for transfers between devices, exchange_rows(): parts = lax.all_to_all(copies, DP, 0, 0, tiled=False)  84.7 us
    ppermute x18, starting transfers between devices, from_behind(): return lax.ppermute(block, axis, route)  68.3 us
    reduce_scatter x1, waiting for transfers between devices, scatter_in_stages(): inner = lax.psum_scatter(block, 'y', scatter_dimension=0, tiled=True)  62.9 us
    all_to_all x1, blocking collectives, supply_block_in(): jax.lax.all_to_all(jnp.stack([w_in] * jax.lax.axis_size('z')), axis_name=...  34.3 us
    all_to_all x1, waiting for transfers between devices, scatter_by_exchange(): arrived = lax.all_to_all(parts, DP, 0, 0, tiled=False)  21.4 us
    reduce_scatter x1, waiting for transfers between devices, scatter_in_stages(): lax.psum_scatter(inner, 'z', scatter_dimension=0, tiled=True)  21.3 us
    psum x1, blocking collectives, on_device(): total_squares = lax.psum(partial_squares, 'section')  18.2 us
  transfers between devices with their start and end apart: 23, of which 22 were waited for; matrix products, arithmetic and copies ran while one was open for 3% of the time, Pallas kernels for 0%

profile of v1, /device:TPU:2, one launch (start us, length us, event | category | flops | bytes accessed | tf_op | source)
XLA Modules:
  0.0 548.8 jit_solution(6434927749698815386)
XLA Ops:
  8.2 34.3 %all_to_all.15 = bf16[8,56,1024]{2,1,0:T(8,128)(2,1)} all-to-all(bf16[8,56,1024]{2,1,0:T(8,128)(2,1)S(1)} %stack.3), channel_id=1, replica_groups=mesh['section'=8,'y'=4,'z'=8] {'z'}, dimensions={0} | all-to-all | bytes 1835008 | tf_op jit(solution)/shard_map/all_to_all | solution.py:167
  42.5 3.2 broadcast_in_dim.63
  45.7 5.1 all-to-all-start.1
  51.6 84.7 %all-to-all-done.1 = bf16[32,32,1792]{2,1,0:T(8,128)(2,1)} async-done(((bf16[32,32,1792]{2,1,0:T(8,128)(2,1)}), bf16[32,32,1792]{2,1,0:T(8,128)(2,1)}, u32[]{:S(2)}, u32[]{:S(2)}) %all-to-all-start.1) | async-done | bytes 3670048 | tf_op jit(solution)/shard_map/all_to_all | solution.py:183
  136.4 91.9 %while.39 = (s32[]{:T(128)}, bf16[64,1792]{1,0:T(8,128)(2,1)S(1)}, bf16[2,64,1792]{2,1,0:T(8,128)(2,1)S(1)}, bf16[2,64,1024]{2,1,0:T(8,128)(2,1)S(1)}, s32[]{:T(...) while((s32[]{:T(128)}, bf16[64,1792]{1,0:T(8,128)(2,1)S(1)}, ...), condition=%wide.region_4.5_spmd, body=%wide.region_0.4_spmd.sunk | while | flops 471269440 | bytes 11721002 | solution.py:91
  137.3 1.9 collective-permute-start
  139.3 5.3 collective-permute-done
  145.4 1.9 collective-permute-start
  147.4 10.9 %collective-permute-done = bf16[64,1792]{1,0:T(8,128)(2,1)S(1)} collective-permute-done((bf16[64,1792]{1,0:T(8,128)(2,1)S(1)}, bf16[64,1792]{1,0:T(8,128)(2,1)S(1)}, u32[]{:S(2)}, u32[]{:S(2)}) %collective-permute-start) | collective-permute-done | bytes 229408 | tf_op jit(solution)/shard_map/while/body/eval_jaxpr/ppermute | solution.py:11
  158.5 6.6 %conditional.4 = (bf16[64,1024]{1,0:T(8,128)(2,1)}, bf16[64,1792]{1,0:T(8,128)(2,1)S(1)}) conditional(s32[]{:T(128)} %convert_element_type.145, () %tuple.96, (bf16[64,1792]{1,0:T(8,128)(2,1)S(1)}, f32[1,1792]{1,0:T(1,128)S(1)}, bf16[1792,1024]{1,0:T(8,128)(2,1)}, bf16[1024,1792]{1,0:T(8,128)(2,1)}) %tuple.97), branch_computations={%region_1.1_spmd, %region_2.3_spmd} | conditional | flops 470974528 | bytes 8542228 | solution.py:74
  158.7 3.5 convolution_convert_fusion
  162.2 2.9 fusion
  165.1 1.9 collective-permute-start
  168.0 4.4 collective-permute-done
  172.5 6.6 %conditional.4 = (bf16[64,1024]{1,0:T(8,128)(2,1)}, bf16[64,1792]{1,0:T(8,128)(2,1)S(1)}) conditional(s32[]{:T(128)} %convert_element_type.145, () %tuple.96, (bf16[64,1792]{1,0:T(8,128)(2,1)S(1)}, f32[1,1792]{1,0:T(1,128)S(1)}, bf16[1792,1024]{1,0:T(8,128)(2,1)}, bf16[1024,1792]{1,0:T(8,128)(2,1)}) %tuple.97), branch_computations={%region_1.1_spmd, %region_2.3_spmd} | conditional | flops 470974528 | bytes 8542228 | solution.py:74
  172.8 3.5 convolution_convert_fusion
  176.3 2.9 fusion
  179.1 1.9 collective-permute-start
  182.0 4.4 collective-permute-done
  187.3 3.8 collective-permute-start
  191.2 3.4 collective-permute-done
  195.5 1.9 collective-permute-start
  197.5 5.3 collective-permute-done
  203.6 7.3 %collective-permute-start = (bf16[64,1792]{1,0:T(8,128)(2,1)S(1)}, bf16[64,1792]{1,0:T(8,128)(2,1)S(1)}, u32[]{:S(2)}, u32[]{:S(2)}) collective-permute-start(bf16[64,1792]{1,0:T(8,128)(2,1)S(1)} %get-tuple-element.751), channel_id=1, source_target_pairs={{0,32},{32,64},{64,96},{96,128},{128,160},{160,192},{192,224},{1,3... | collective-permute-start | bytes 688136 | tf_op jit(solution)/shard_map/while/body/eval_jaxpr/ppermute | solution.py:11
  212.8 6.2 %collective-permute-start = (bf16[64,1792]{1,0:T(8,128)(2,1)S(1)}, bf16[64,1792]{1,0:T(8,128)(2,1)S(1)}, u32[]{:S(2)}, u32[]{:S(2)}) collective-permute-start(bf16[64,1792]{1,0:T(8,128)(2,1)S(1)} %get-tuple-element.751), channel_id=1, source_target_pairs={{0,32},{32,64},{64,96},{96,128},{128,160},{160,192},{192,224},{1,3... | collective-permute-start | bytes 688136 | tf_op jit(solution)/shard_map/while/body/eval_jaxpr/ppermute | solution.py:11
  221.0 6.2 %collective-permute-start = (bf16[64,1792]{1,0:T(8,128)(2,1)S(1)}, bf16[64,1792]{1,0:T(8,128)(2,1)S(1)}, u32[]{:S(2)}, u32[]{:S(2)}) collective-permute-start(bf16[64,1792]{1,0:T(8,128)(2,1)S(1)} %get-tuple-element.751), channel_id=1, source_target_pairs={{0,32},{32,64},{64,96},{96,128},{128,160},{160,192},{192,224},{1,3... | collective-permute-start | bytes 688136 | tf_op jit(solution)/shard_map/while/body/eval_jaxpr/ppermute | solution.py:11
  228.6 172.9 %while.40 = (s32[]{:T(128)}, bf16[64,1792]{1,0:T(8,128)(2,1)S(1)}, bf16[2,64,1792]{2,1,0:T(8,128)(2,1)S(1)}, bf16[2,64,1024]{2,1,0:T(8,128)(2,1)S(1)}, f32[2,1]{...) while((s32[]{:T(128)}, bf16[64,1792]{1,0:T(8,128)(2,1)S(1)}, ...), condition=%wide.region_13.14_spmd, body=%wide.region_6.0_spmd.sunk | while | flops 949518400 | bytes 14876903 | solution.py:156
  228.8 1.9 collective-permute-start.1
  232.1 3.9 collective-permute-done.1
  236.2 2.0 collective-permute-start.1
  239.7 5.7 %collective-permute-done.1 = bf16[64,1792]{1,0:T(8,128)(2,1)S(1)} collective-permute-done((bf16[64,1792]{1,0:T(8,128)(2,1)S(1)}, bf16[64,1792]{1,0:T(8,128)(2,1)S(1)}, u32[]{:S(2)}, u32[]{:S(2)}) %collective-permute-start.1) | collective-permute-done | bytes 229408 | tf_op jit(solution)/shard_map/while/body/eval_jaxpr/ppermute | solution.py:11
  245.6 1.9 collective-permute-start.1
  248.8 4.1 collective-permute-done.1
  253.1 1.9 collective-permute-start.1
  256.4 4.7 collective-permute-done.1
  261.3 1.9 collective-permute-start.1
  264.5 66.8 %collective-permute-done.1 = bf16[64,1792]{1,0:T(8,128)(2,1)S(1)} collective-permute-done((bf16[64,1792]{1,0:T(8,128)(2,1)S(1)}, bf16[64,1792]{1,0:T(8,128)(2,1)S(1)}, u32[]{:S(2)}, u32[]{:S(2)}) %collective-permute-start.1) | collective-permute-done | bytes 229408 | tf_op jit(solution)/shard_map/while/body/eval_jaxpr/ppermute | solution.py:11
  331.5 14.0 %conditional.5 = (bf16[64,1792]{1,0:T(8,128)(2,1)S(1)}, bf16[64,1024]{1,0:T(8,128)(2,1)S(1)}, f32[1]{0:T(128)}) conditional(s32[]{:T(128)} %convert_element_type.146, () %tuple.100, (bf16[64,1792]{1,0:T(8,128)(2,1)S(1)}, bf16[2,64,1792]{2,1,0:T(8,128)(2,1)S(1)}, s32[]{:T(128)}, bf16[1024,1792]{1,0:T(8,128)(2,1)}, bf16[1792,1024]{1,0:T(8,128)(2,1)}, ...), branch_computations={%region_7.7_spmd, %region_8.12_spmd} | conditional | flops 949223488 | bytes 11698044 | solution.py:132
  331.6 3.3 convolution_convert_fusion.1
  335.0 3.4 fusion.10
  338.6 2.8 multiply_reduce_fusion.1
  341.4 2.8 multiply_reduce_fusion
  345.5 1.9 collective-permute-start.1
  348.8 4.1 collective-permute-done.1
  353.0 14.0 %conditional.5 = (bf16[64,1792]{1,0:T(8,128)(2,1)S(1)}, bf16[64,1024]{1,0:T(8,128)(2,1)S(1)}, f32[1]{0:T(128)}) conditional(s32[]{:T(128)} %convert_element_type.146, () %tuple.100, (bf16[64,1792]{1,0:T(8,128)(2,1)S(1)}, bf16[2,64,1792]{2,1,0:T(8,128)(2,1)S(1)}, s32[]{:T(128)}, bf16[1024,1792]{1,0:T(8,128)(2,1)}, bf16[1792,1024]{1,0:T(8,128)(2,1)}, ...), branch_computations={%region_7.7_spmd, %region_8.12_spmd} | conditional | flops 949223488 | bytes 11698044 | solution.py:132
  353.2 3.3 convolution_convert_fusion.1
  356.5 3.4 fusion.10
  360.1 2.8 multiply_reduce_fusion.1
  362.9 2.8 multiply_reduce_fusion
  367.0 1.9 collective-permute-start.1
  370.4 2.1 collective-permute-done.1
  372.7 17.8 %collective-permute-start.1 = (bf16[64,1792]{1,0:T(8,128)(2,1)S(1)}, bf16[64,1792]{1,0:T(8,128)(2,1)S(1)}, u32[]{:S(2)}, u32[]{:S(2)}) collective-permute-start(bf16[64,1792]{1,0:T(8,128)(2,1)S(1)} %get-tuple-element.768), channel_id=1, source_target_pairs={{32,0},{64,32},{96,64},{128,96},{160,128},{192,160},{224,192},{33,... | collective-permute-start | bytes 688136 | tf_op jit(solution)/shard_map/while/body/eval_jaxpr/ppermute | solution.py:11
  391.9 2.1 collective-permute-done.1
  394.2 3.8 collective-permute-start.1
  399.4 2.1 collective-permute-done.1
  401.5 18.2 %psum.7 = f32[2,1]{0,1:T(1,128)S(1)} all-reduce(f32[2,1]{0,1:T(1,128)S(1)} %get-tuple-element.560), channel_id=1, replica_groups=mesh['section'=8,'y'=4,'z'=8] {'section'}, use_global_device_ids=true, to_apply=%region_14.15 | all-reduce | flops 2 | bytes 16 | tf_op jit(solution)/shard_map/psum | solution.py:211
  419.7 3.1 bitcast_convert_fusion.1
  422.9 3.1 bitcast_convert_fusion
  426.0 5.7 %all-to-all-start.2 = ((bf16[32,32,1792]{2,1,0:T(8,128)(2,1)}), bf16[32,32,1792]{2,1,0:T(8,128)(2,1)}, u32[]{:S(2)}, u32[]{:S(2)}) async-start(bf16[32,32,1792]{2,1,0:T(8,128)(2,1)} %bitcast.99), calls=%async_computation.4 | async-start | bytes 7340032 | tf_op jit(solution)/shard_map/all_to_all | solution.py:195
  431.7 62.9 %reduce-scatter.3.cloned.1.call-done = bf16[448,1024]{1,0:T(8,128)(2,1)} async-done(((bf16[1792,1024]{1,0:T(8,128)(2,1)}), bf16[448,1024]{1,0:T(8,128)(2,1)}) %reduce-scatter.3.cloned.1.call-update) | async-done | bytes 917520 | tf_op jit(solution)/shard_map/reduce_scatter | solution.py:188
  494.7 21.4 %all-to-all-done.2 = bf16[32,32,1792]{2,1,0:T(8,128)(2,1)} async-done(((bf16[32,32,1792]{2,1,0:T(8,128)(2,1)}), bf16[32,32,1792]{2,1,0:T(8,128)(2,1)}, u32[]{:S(2)}, u32[]{:S(2)}) %all-to-all-start.2) | async-done | bytes 3670048 | tf_op jit(solution)/shard_map/all_to_all | solution.py:195
  516.1 2.6 convert_reduce_fusion
  519.4 21.3 %reduce-scatter.5.cloned.1.call-done = bf16[56,1024]{1,0:T(8,128)(2,1)} async-done(((bf16[448,1024]{1,0:T(8,128)(2,1)}), bf16[56,1024]{1,0:T(8,128)(2,1)}) %reduce-scatter.5.cloned.1.call-update) | async-done | bytes 114704 | tf_op jit(solution)/shard_map/reduce_scatter | solution.py:189
  540.7 1.6 fusion.34
  (189 shorter events, 28.5 us)
Async XLA Ops:
  45.7 5.9 %copy-start.4 = (f32[1,1792]{1,0:T(1,128)S(1)}, f32[1,1792]{1,0:T(1,128)}, u32[]{:S(2)}) copy-start(f32[1,1792]{1,0:T(1,128)} %param.19) | copy-start | bytes 21508
  45.7 90.7 %copy-start.2 = (bf16[2,1,64,1792]{3,2,1,0:T(8,128)(2,1)S(1)}, bf16[2,1,64,1792]{3,2,1,0:T(8,128)(2,1)}, u32[]{:S(2)}) copy-start(bf16[2,1,64,1792]{3,2,1,0:T(8,128)(2,1)} %param.15) | copy-start | bytes 1376260
  45.7 90.6 %all-to-all-start.1 = ((bf16[32,32,1792]{2,1,0:T(8,128)(2,1)}), bf16[32,32,1792]{2,1,0:T(8,128)(2,1)}, u32[]{:S(2)}, u32[]{:S(2)}) async-start(bf16[32,32,1792]{2,1,0:T(8,128)(2,1)} %broadcast_in_dim.63), calls=%async_computation.1 | async-start | bytes 7340032 | tf_op jit(solution)/shard_map/all_to_all | solution.py:183
  50.8 85.5 %all-gather.2.cloned.1.call-start = ((), (), s32[]{:S(2)}) async-start(), calls=%async_computation.5 | async-start | bytes 4587520 | tf_op jit(solution)/shard_map/all_gather | solution.py:177
  51.5 443.1 %reduce-scatter.3.cloned.1.call-start = ((), (), s32[]{:S(2)}) async-start(), calls=%async_computation.6 | async-start | bytes 4587520 | tf_op jit(solution)/shard_map/reduce_scatter | solution.py:188
  136.4 92.2 %copy-start.3 = (bf16[2,1,64,1792]{3,2,1,0:T(8,128)(2,1)S(1)}, bf16[2,1,64,1792]{3,2,1,0:T(8,128)(2,1)}, u32[]{:S(2)}) copy-start(bf16[2,1,64,1792]{3,2,1,0:T(8,128)(2,1)} %param.16) | copy-start | bytes 1376260
  137.3 7.3 %collective-permute-start = (bf16[64,1792]{1,0:T(8,128)(2,1)S(1)}, bf16[64,1792]{1,0:T(8,128)(2,1)S(1)}, u32[]{:S(2)}, u32[]{:S(2)}) collective-permute-start(bf16[64,1792]{1,0:T(8,128)(2,1)S(1)} %get-tuple-element.751), channel_id=1, source_target_pairs={{0,32},{32,64},{64,96},{96,128},{128,160},{160,192},{192,224},{1,3... | collective-permute-start | bytes 688136 | tf_op jit(solution)/shard_map/while/body/eval_jaxpr/ppermute | solution.py:11
  145.4 12.9 %collective-permute-start = (bf16[64,1792]{1,0:T(8,128)(2,1)S(1)}, bf16[64,1792]{1,0:T(8,128)(2,1)S(1)}, u32[]{:S(2)}, u32[]{:S(2)}) collective-permute-start(bf16[64,1792]{1,0:T(8,128)(2,1)S(1)} %get-tuple-element.751), channel_id=1, source_target_pairs={{0,32},{32,64},{64,96},{96,128},{128,160},{160,192},{192,224},{1,3... | collective-permute-start | bytes 688136 | tf_op jit(solution)/shard_map/while/body/eval_jaxpr/ppermute | solution.py:11
  165.1 7.3 %collective-permute-start = (bf16[64,1792]{1,0:T(8,128)(2,1)S(1)}, bf16[64,1792]{1,0:T(8,128)(2,1)S(1)}, u32[]{:S(2)}, u32[]{:S(2)}) collective-permute-start(bf16[64,1792]{1,0:T(8,128)(2,1)S(1)} %get-tuple-element.751), channel_id=1, source_target_pairs={{0,32},{32,64},{64,96},{96,128},{128,160},{160,192},{192,224},{1,3... | collective-permute-start | bytes 688136 | tf_op jit(solution)/shard_map/while/body/eval_jaxpr/ppermute | solution.py:11
  179.1 7.3 %collective-permute-start = (bf16[64,1792]{1,0:T(8,128)(2,1)S(1)}, bf16[64,1792]{1,0:T(8,128)(2,1)S(1)}, u32[]{:S(2)}, u32[]{:S(2)}) collective-permute-start(bf16[64,1792]{1,0:T(8,128)(2,1)S(1)} %get-tuple-element.751), channel_id=1, source_target_pairs={{0,32},{32,64},{64,96},{96,128},{128,160},{160,192},{192,224},{1,3... | collective-permute-start | bytes 688136 | tf_op jit(solution)/shard_map/while/body/eval_jaxpr/ppermute | solution.py:11
  187.3 7.3 %collective-permute-start = (bf16[64,1792]{1,0:T(8,128)(2,1)S(1)}, bf16[64,1792]{1,0:T(8,128)(2,1)S(1)}, u32[]{:S(2)}, u32[]{:S(2)}) collective-permute-start(bf16[64,1792]{1,0:T(8,128)(2,1)S(1)} %get-tuple-element.751), channel_id=1, source_target_pairs={{0,32},{32,64},{64,96},{96,128},{128,160},{160,192},{192,224},{1,3... | collective-permute-start | bytes 688136 | tf_op jit(solution)/shard_map/while/body/eval_jaxpr/ppermute | solution.py:11
  195.5 7.3 %collective-permute-start = (bf16[64,1792]{1,0:T(8,128)(2,1)S(1)}, bf16[64,1792]{1,0:T(8,128)(2,1)S(1)}, u32[]{:S(2)}, u32[]{:S(2)}) collective-permute-start(bf16[64,1792]{1,0:T(8,128)(2,1)S(1)} %get-tuple-element.751), channel_id=1, source_target_pairs={{0,32},{32,64},{64,96},{96,128},{128,160},{160,192},{192,224},{1,3... | collective-permute-start | bytes 688136 | tf_op jit(solution)/shard_map/while/body/eval_jaxpr/ppermute | solution.py:11
  203.6 8.4 %collective-permute-start = (bf16[64,1792]{1,0:T(8,128)(2,1)S(1)}, bf16[64,1792]{1,0:T(8,128)(2,1)S(1)}, u32[]{:S(2)}, u32[]{:S(2)}) collective-permute-start(bf16[64,1792]{1,0:T(8,128)(2,1)S(1)} %get-tuple-element.751), channel_id=1, source_target_pairs={{0,32},{32,64},{64,96},{96,128},{128,160},{160,192},{192,224},{1,3... | collective-permute-start | bytes 688136 | tf_op jit(solution)/shard_map/while/body/eval_jaxpr/ppermute | solution.py:11
  212.8 7.3 %collective-permute-start = (bf16[64,1792]{1,0:T(8,128)(2,1)S(1)}, bf16[64,1792]{1,0:T(8,128)(2,1)S(1)}, u32[]{:S(2)}, u32[]{:S(2)}) collective-permute-start(bf16[64,1792]{1,0:T(8,128)(2,1)S(1)} %get-tuple-element.751), channel_id=1, source_target_pairs={{0,32},{32,64},{64,96},{96,128},{128,160},{160,192},{192,224},{1,3... | collective-permute-start | bytes 688136 | tf_op jit(solution)/shard_map/while/body/eval_jaxpr/ppermute | solution.py:11
  221.0 7.3 %collective-permute-start = (bf16[64,1792]{1,0:T(8,128)(2,1)S(1)}, bf16[64,1792]{1,0:T(8,128)(2,1)S(1)}, u32[]{:S(2)}, u32[]{:S(2)}) collective-permute-start(bf16[64,1792]{1,0:T(8,128)(2,1)S(1)} %get-tuple-element.751), channel_id=1, source_target_pairs={{0,32},{32,64},{64,96},{96,128},{128,160},{160,192},{192,224},{1,3... | collective-permute-start | bytes 688136 | tf_op jit(solution)/shard_map/while/body/eval_jaxpr/ppermute | solution.py:11
  228.8 7.2 %collective-permute-start.1 = (bf16[64,1792]{1,0:T(8,128)(2,1)S(1)}, bf16[64,1792]{1,0:T(8,128)(2,1)S(1)}, u32[]{:S(2)}, u32[]{:S(2)}) collective-permute-start(bf16[64,1792]{1,0:T(8,128)(2,1)S(1)} %get-tuple-element.768), channel_id=1, source_target_pairs={{32,0},{64,32},{96,64},{128,96},{160,128},{192,160},{224,192},{33,... | collective-permute-start | bytes 688136 | tf_op jit(solution)/shard_map/while/body/eval_jaxpr/ppermute | solution.py:11
  236.2 9.1 %collective-permute-start.1 = (bf16[64,1792]{1,0:T(8,128)(2,1)S(1)}, bf16[64,1792]{1,0:T(8,128)(2,1)S(1)}, u32[]{:S(2)}, u32[]{:S(2)}) collective-permute-start(bf16[64,1792]{1,0:T(8,128)(2,1)S(1)} %get-tuple-element.768), channel_id=1, source_target_pairs={{32,0},{64,32},{96,64},{128,96},{160,128},{192,160},{224,192},{33,... | collective-permute-start | bytes 688136 | tf_op jit(solution)/shard_map/while/body/eval_jaxpr/ppermute | solution.py:11
  245.6 7.3 %collective-permute-start.1 = (bf16[64,1792]{1,0:T(8,128)(2,1)S(1)}, bf16[64,1792]{1,0:T(8,128)(2,1)S(1)}, u32[]{:S(2)}, u32[]{:S(2)}) collective-permute-start(bf16[64,1792]{1,0:T(8,128)(2,1)S(1)} %get-tuple-element.768), channel_id=1, source_target_pairs={{32,0},{64,32},{96,64},{128,96},{160,128},{192,160},{224,192},{33,... | collective-permute-start | bytes 688136 | tf_op jit(solution)/shard_map/while/body/eval_jaxpr/ppermute | solution.py:11
  253.1 8.0 %collective-permute-start.1 = (bf16[64,1792]{1,0:T(8,128)(2,1)S(1)}, bf16[64,1792]{1,0:T(8,128)(2,1)S(1)}, u32[]{:S(2)}, u32[]{:S(2)}) collective-permute-start(bf16[64,1792]{1,0:T(8,128)(2,1)S(1)} %get-tuple-element.768), channel_id=1, source_target_pairs={{32,0},{64,32},{96,64},{128,96},{160,128},{192,160},{224,192},{33,... | collective-permute-start | bytes 688136 | tf_op jit(solution)/shard_map/while/body/eval_jaxpr/ppermute | solution.py:11
  261.3 70.1 %collective-permute-start.1 = (bf16[64,1792]{1,0:T(8,128)(2,1)S(1)}, bf16[64,1792]{1,0:T(8,128)(2,1)S(1)}, u32[]{:S(2)}, u32[]{:S(2)}) collective-permute-start(bf16[64,1792]{1,0:T(8,128)(2,1)S(1)} %get-tuple-element.768), channel_id=1, source_target_pairs={{32,0},{64,32},{96,64},{128,96},{160,128},{192,160},{224,192},{33,... | collective-permute-start | bytes 688136 | tf_op jit(solution)/shard_map/while/body/eval_jaxpr/ppermute | solution.py:11
  334.9 6.5 %copy-start = (bf16[64,1024]{1,0:T(8,128)(2,1)}, bf16[64,1024]{1,0:T(8,128)(2,1)S(1)}, u32[]{:S(2)}) copy-start(bf16[64,1024]{1,0:T(8,128)(2,1)S(1)} %convolution_convert_fusion.1) | copy-start | bytes 393220 | tf_op jit(solution)/shard_map/while/body/eval_jaxpr/cond
  341.4 4.1 copy-start.1
  345.5 7.3 %collective-permute-start.1 = (bf16[64,1792]{1,0:T(8,128)(2,1)S(1)}, bf16[64,1792]{1,0:T(8,128)(2,1)S(1)}, u32[]{:S(2)}, u32[]{:S(2)}) collective-permute-start(bf16[64,1792]{1,0:T(8,128)(2,1)S(1)} %get-tuple-element.768), channel_id=1, source_target_pairs={{32,0},{64,32},{96,64},{128,96},{160,128},{192,160},{224,192},{33,... | collective-permute-start | bytes 688136 | tf_op jit(solution)/shard_map/while/body/eval_jaxpr/ppermute | solution.py:11
  356.4 6.5 %copy-start = (bf16[64,1024]{1,0:T(8,128)(2,1)}, bf16[64,1024]{1,0:T(8,128)(2,1)S(1)}, u32[]{:S(2)}) copy-start(bf16[64,1024]{1,0:T(8,128)(2,1)S(1)} %convolution_convert_fusion.1) | copy-start | bytes 393220 | tf_op jit(solution)/shard_map/while/body/eval_jaxpr/cond
  362.9 4.1 copy-start.1
  367.0 5.4 collective-permute-start.1
  372.7 21.3 %collective-permute-start.1 = (bf16[64,1792]{1,0:T(8,128)(2,1)S(1)}, bf16[64,1792]{1,0:T(8,128)(2,1)S(1)}, u32[]{:S(2)}, u32[]{:S(2)}) collective-permute-start(bf16[64,1792]{1,0:T(8,128)(2,1)S(1)} %get-tuple-element.768), channel_id=1, source_target_pairs={{32,0},{64,32},{96,64},{128,96},{160,128},{192,160},{224,192},{33,... | collective-permute-start | bytes 688136 | tf_op jit(solution)/shard_map/while/body/eval_jaxpr/ppermute | solution.py:11
  394.2 7.3 %collective-permute-start.1 = (bf16[64,1792]{1,0:T(8,128)(2,1)S(1)}, bf16[64,1792]{1,0:T(8,128)(2,1)S(1)}, u32[]{:S(2)}, u32[]{:S(2)}) collective-permute-start(bf16[64,1792]{1,0:T(8,128)(2,1)S(1)} %get-tuple-element.768), channel_id=1, source_target_pairs={{32,0},{64,32},{96,64},{128,96},{160,128},{192,160},{224,192},{33,... | collective-permute-start | bytes 688136 | tf_op jit(solution)/shard_map/while/body/eval_jaxpr/ppermute | solution.py:11
  426.0 90.1 %all-to-all-start.2 = ((bf16[32,32,1792]{2,1,0:T(8,128)(2,1)}), bf16[32,32,1792]{2,1,0:T(8,128)(2,1)}, u32[]{:S(2)}, u32[]{:S(2)}) async-start(bf16[32,32,1792]{2,1,0:T(8,128)(2,1)} %bitcast.99), calls=%async_computation.4 | async-start | bytes 7340032 | tf_op jit(solution)/shard_map/all_to_all | solution.py:195
  431.7 87.0 %copy-start.6 = (f32[1,32,1792]{2,1,0:T(8,128)S(1)}, f32[1,32,1792]{2,1,0:T(8,128)}, u32[]{:S(2)}) copy-start(f32[1,32,1792]{2,1,0:T(8,128)} %param.21) | copy-start | bytes 688132
  431.7 109.0 %copy-start.5 = (f32[1,56,1024]{2,1,0:T(8,128)S(1)}, f32[1,56,1024]{2,1,0:T(8,128)}, u32[]{:S(2)}) copy-start(f32[1,56,1024]{2,1,0:T(8,128)} %param.20) | copy-start | bytes 688132
  431.7 109.0 %reduce-scatter.5.cloned.1.call-start = ((), (), s32[]{:S(2)}) async-start(), calls=%async_computation.7 | async-start | bytes 1032192 | tf_op jit(solution)/shard_map/reduce_scatter | solution.py:189
Sparse Core Ops, SparseCore 0:
  53.5 74.0 all-gather.1
  423.0 71.6 reduce-scatter.2
  497.2 43.3 reduce-scatter.4
